TPU v7x, 32 devices: a whole 2x2x4 slice. The times are simulated.
32 devices in a mesh: groups: 2 (over y), seq: 8 (over z, x), tensor: 2 (over core).
Axes of the slice: x: 2, y: 2, z: 4, core: 2. Of those that a mesh axis runs over, the one named last changes fastest.
Arguments:
- queries: bfloat16 [4, 1024, 2048], P(('groups', 'tensor'), 'seq'), parts along dimension 0, may hold values from -33 to 33
- keys: bfloat16 [4, 1024, 2048], P(('groups', 'tensor'), 'seq'), parts along dimension 0, may hold values from -33 to 33
- values: bfloat16 [4, 1024, 2048], P(('groups', 'tensor'), 'seq'), parts along dimension 0, may hold values from -6 to 6
- out_grad: bfloat16 [4, 1024, 2048], P(('groups', 'tensor'), 'seq'), parts along dimension 0, may hold values from -96 to 96
- tile_lists: int32 [32, 12], P(('groups', 'tensor')), parts along dimension 0, may hold values from -1 to 15, as said below
Outputs:
- query_grad: bfloat16 [4, 1024, 2048], P(('groups', 'tensor'), 'seq'), parts along dimension 0
- key_grad: bfloat16 [4, 1024, 2048], P(('groups', 'tensor'), 'seq'), parts along dimension 0
- value_grad: bfloat16 [4, 1024, 2048], P(('groups', 'tensor'), 'seq'), parts along dimension 0
There are 2 independent parts, one for each index of `groups`. A program takes and returns all parts, laid end to end along the dimension named above; each array names one. Nothing has to cross between parts.
Inputs may be any that keep to these rules, and one draw needn't show every extreme that they name: `tile_lists`: row i begins with i; its other entries are distinct tiles within 8 of i, followed by -1 entries only where fewer such tiles lie inside the clip.
All inputs are finite; a program needn't handle non-finite values.
Results may differ from a plain program's by a relative error of at most 0.012.
Values may be sent and summed in bfloat16 or wider, within the bound.
A program may use at most 128 MiB of HBM per device.

v0:
```python
import math

import jax
import jax.numpy as jnp
from jax import lax
from jax.sharding import PartitionSpec as P

HEADS = 16
DH = 128
TILE = 128
RADIUS = 8
WIN = 12


block_tiles = 4


def padded_2(block, sides, width):
    for axis, dim in sides:
        count = lax.axis_size(axis)
        forward = [(i, i + 1) for i in range(count - 1)]
        backward = [(target, source) for source, target in forward]
        low = lax.ppermute(
            lax.slice_in_dim(block, block.shape[dim] - width, None, axis=dim), axis, forward
        )
        high = lax.ppermute(lax.slice_in_dim(block, 0, width, axis=dim), axis, backward)
        block = jnp.concatenate([low, block, high], axis=dim)
    return block


def key_rims(key_rows, value_rows):
    joined = jnp.concatenate([key_rows, value_rows], 1)
    return padded_2(joined, (("tensor", 0),), RADIUS * TILE)


def finish_rims(grads_ext, segment, local_width):
    rim_rows = RADIUS * TILE
    outer_rows = jnp.concatenate([grads_ext[:rim_rows], grads_ext[-rim_rows:]], 0)
    arrived = padded_2(outer_rows, (("tensor", 0),), rim_rows)
    own_rows = grads_ext[rim_rows : rim_rows + segment]
    own_rows = own_rows.at[:rim_rows].add(arrived[:rim_rows])
    own_rows = own_rows.at[segment - rim_rows :].add(arrived[3 * rim_rows :])
    own_rows = own_rows.astype(jnp.bfloat16)
    return (own_rows[:, :local_width], own_rows[:, local_width:])


def body(queries, keys, values, out_grad, tile_lists):
    span_rows = queries.shape[1]
    feature_count = queries.shape[2]
    seq_count = lax.axis_size("seq")
    heads_here = HEADS // seq_count
    local_width = heads_here * DH
    score_scale = 1.0 / math.sqrt(DH)
    query_tokens = queries.reshape(span_rows, feature_count)
    key_tokens = keys.reshape(span_rows, feature_count)
    value_tokens = values.reshape(span_rows, feature_count)
    grad_tokens = out_grad.reshape(span_rows, feature_count)
    query_rows, key_rows, value_rows, grad_rows = (
        lax.all_to_all(query_tokens, "seq", split_axis=1, concat_axis=0, tiled=True),
        lax.all_to_all(key_tokens, "seq", split_axis=1, concat_axis=0, tiled=True),
        lax.all_to_all(value_tokens, "seq", split_axis=1, concat_axis=0, tiled=True),
        lax.all_to_all(grad_tokens, "seq", split_axis=1, concat_axis=0, tiled=True),
    )
    padded = key_rims(key_rows, value_rows)
    segment = query_rows.shape[0]
    seg_tiles = segment // TILE
    ext_tiles = seg_tiles + 2 * RADIUS
    block_count = seg_tiles // block_tiles
    first_tile = lax.axis_index("tensor") * seg_tiles - RADIUS
    kv_tiles = padded.reshape(ext_tiles, TILE, 2 * local_width)
    query_blocks = query_rows.reshape(block_count, block_tiles, TILE, heads_here, DH)
    grad_blocks = grad_rows.reshape(block_count, block_tiles, TILE, heads_here, DH)
    list_blocks = tile_lists.reshape(block_count, block_tiles, WIN)

    def attend_block(totals, inputs):
        query_block, grad_block, tile_rows = inputs
        present = tile_rows >= 0
        local_tile = jnp.clip(tile_rows - first_tile, 0, ext_tiles - 1)
        picked = kv_tiles[local_tile].reshape(block_tiles, WIN * TILE, 2, heads_here, DH)
        key_sel = picked[:, :, 0]
        value_sel = picked[:, :, 1]
        scores = (
            jnp.einsum("gthd,gkhd->ghtk", query_block, key_sel, preferred_element_type=jnp.float32)
            * score_scale
        )
        live_keys = jnp.repeat(present, TILE, axis=1)
        scores = jnp.where(live_keys[:, None, None, :], scores, -1e30)
        row_max = jnp.max(scores, axis=3, keepdims=True)
        weights = jnp.exp(scores - row_max)
        weights = weights / jnp.sum(weights, axis=3, keepdims=True)
        weights_b = weights.astype(jnp.bfloat16)
        recomputed = jnp.einsum(
            "ghtk,gkhd->gthd", weights_b, value_sel, preferred_element_type=jnp.float32
        )
        delta = jnp.sum(grad_block.astype(jnp.float32) * recomputed, axis=3)
        prob_grad = jnp.einsum(
            "gthd,gkhd->ghtk", grad_block, value_sel, preferred_element_type=jnp.float32
        )
        score_grad = (
            weights * (prob_grad - jnp.transpose(delta, (0, 2, 1))[..., None]) * score_scale
        ).astype(jnp.bfloat16)
        query_part = jnp.einsum(
            "ghtk,gkhd->gthd", score_grad, key_sel, preferred_element_type=jnp.float32
        ).astype(jnp.bfloat16)
        key_part = jnp.einsum(
            "ghtk,gthd->gkhd", score_grad, query_block, preferred_element_type=jnp.float32
        )
        value_part = jnp.einsum(
            "ghtk,gthd->gkhd", weights_b, grad_block, preferred_element_type=jnp.float32
        )
        key_terms = jnp.concatenate([key_part, value_part], 2).reshape(
            block_tiles, WIN, TILE, 2 * local_width
        )
        totals = totals.at[local_tile].add(key_terms)
        return (totals, query_part)

    initial = jnp.zeros((ext_tiles, TILE, 2 * local_width), jnp.float32)
    grads_ext, query_parts = lax.scan(
        attend_block, initial, (query_blocks, grad_blocks, list_blocks)
    )
    query_grad = query_parts.reshape(segment, local_width)
    grads_ext = grads_ext.reshape(ext_tiles * TILE, 2 * local_width)
    query_back = lax.all_to_all(query_grad, "seq", split_axis=0, concat_axis=1, tiled=True)
    key_grad, value_grad = finish_rims(grads_ext, segment, local_width)
    key_back, value_back = (
        lax.all_to_all(key_grad, "seq", split_axis=0, concat_axis=1, tiled=True),
        lax.all_to_all(value_grad, "seq", split_axis=0, concat_axis=1, tiled=True),
    )
    out_shape = queries.shape
    return (
        query_back.reshape(out_shape),
        key_back.reshape(out_shape),
        value_back.reshape(out_shape),
    )


def solution(mesh):
    return jax.shard_map(
        body,
        mesh=mesh,
        in_specs=(
            P(("groups", "tensor"), "seq", None),
            P(("groups", "tensor"), "seq", None),
            P(("groups", "tensor"), "seq", None),
            P(("groups", "tensor"), "seq", None),
            P(("groups", "tensor"), None),
        ),
        out_specs=(
            P(("groups", "tensor"), "seq", None),
            P(("groups", "tensor"), "seq", None),
            P(("groups", "tensor"), "seq", None),
        ),
        check_vma=False,
    )
```

profile of v0, /device:TPU:0, one launch (start us, length us, event | category | flops | bytes accessed | tf_op | source)
XLA Modules:
  0.0 385.2 jit_solution(5358076679016912384)
XLA Ops:
  0.7 1.4 copy.76
  3.1 7.3 %all-to-all-start.1 = ((bf16[128,8,256]{2,0,1:T(8,128)(2,1)}), bf16[128,8,256]{2,0,1:T(8,128)(2,1)S(1)}, u32[]{:S(2)}, u32[]{:S(2)}) async-start(bf16[128,8,256]{2,0,1:T(8,128)(2,1)} %copy.77), calls=%async_computation.1 | async-start | bytes 1048576 | tf_op jit(solution)/shard_map/all_to_all | solution.py:60
  10.3 1.3 copy.78
  12.7 12.2 %all-to-all-done.1 = bf16[128,8,256]{2,0,1:T(8,128)(2,1)S(1)} async-done(((bf16[128,8,256]{2,0,1:T(8,128)(2,1)}), bf16[128,8,256]{2,0,1:T(8,128)(2,1)S(1)}, u32[]{:S(2)}, u32[]{:S(2)}) %all-to-all-start.1) | async-done | bytes 524320 | tf_op jit(solution)/shard_map/all_to_all | solution.py:60
  24.8 3.6 all-to-all-start.2
  29.5 13.7 %all-to-all-done.2 = bf16[128,8,256]{2,0,1:T(8,128)(2,1)S(1)} async-done(((bf16[128,8,256]{2,0,1:T(8,128)(2,1)}), bf16[128,8,256]{2,0,1:T(8,128)(2,1)S(1)}, u32[]{:S(2)}, u32[]{:S(2)}) %all-to-all-start.2) | async-done | bytes 524320 | tf_op jit(solution)/shard_map/all_to_all | solution.py:61
  43.1 3.6 all-to-all-start
  48.2 5.0 %collective-permute-start = (bf16[1024,512]{1,0:T(8,128)(2,1)S(1)}, bf16[1024,512]{1,0:T(8,128)(2,1)}, u32[]{:S(2)}, u32[]{:S(2)}) collective-permute-start(bf16[1024,512]{1,0:T(8,128)(2,1)S(1)} %pad_maximum_fusion.2), channel_id=1, source_target_pairs={{0,1},{2,3},{4,5},{6,7},{8,9},{10,11},{12,13},{14,15},{16,17},{18,... | collective-permute-start | bytes 3145736 | tf_op jit(solution)/shard_map/ppermute | solution.py:23
  54.2 7.3 %all-to-all-done = bf16[128,8,256]{0,2,1:T(8,128)(2,1)S(1)} async-done(((bf16[128,8,256]{0,2,1:T(8,128)(2,1)}), bf16[128,8,256]{0,2,1:T(8,128)(2,1)S(1)}, u32[]{:S(2)}, u32[]{:S(2)}) %all-to-all-start) | async-done | bytes 524320 | tf_op jit(solution)/shard_map/all_to_all | solution.py:59
  61.5 4.1 %all-to-all-start.3 = ((bf16[128,8,256]{0,2,1:T(8,128)(2,1)}), bf16[128,8,256]{0,2,1:T(8,128)(2,1)}, u32[]{:S(2)}, u32[]{:S(2)}) async-start(bf16[128,8,256]{0,2,1:T(8,128)(2,1)} %bitcast.23), calls=%async_computation.3 | async-start | bytes 1048576 | tf_op jit(solution)/shard_map/all_to_all | solution.py:62
  65.7 2.1 pad_maximum_fusion.1
  67.8 12.1 %all-to-all-done.3 = bf16[128,8,256]{0,2,1:T(8,128)(2,1)} async-done(((bf16[128,8,256]{0,2,1:T(8,128)(2,1)}), bf16[128,8,256]{0,2,1:T(8,128)(2,1)}, u32[]{:S(2)}, u32[]{:S(2)}) %all-to-all-start.3) | async-done | bytes 524320 | tf_op jit(solution)/shard_map/all_to_all | solution.py:62
  79.9 3.5 broadcast_in_dim.32
  83.4 235.3 %while.16 = (s32[]{:T(128)}, f32[24,128,512]{2,1,0:T(8,128)}, bf16[2,4,128,2,128]{2,4,3,1,0:T(8,128)(2,1)}, s32[2,4,12]{2,1,0:T(4,128)S(1)}, s32[]{:T(128)}, /*i...) while((s32[]{:T(128)}, f32[24,128,512]{2,1,0:T(8,128)}, ...), condition=%wide.region_5.6_spmd, body=%wide.region_0.5_spmd.sunk | while | flops 2443183872 | bytes 270063488 | solution.py:118
  85.4 4.9 %gather_fusion = bf16[48,128,512]{2,1,0:T(8,128)(2,1)} fusion(bf16[24,128,512]{2,1,0:T(8,128)(2,1)S(1)} %get-tuple-element.235, s32[1024]{0:T(1024)S(1)} %pad_clamp_fusion.2), kind=kCustom, calls=%fused_computation.clone.1 | custom fusion | bytes 12583104 | tf_op jit(solution)/shard_map/while/body/eval_jaxpr/gather | solution.py:79
  90.3 9.7 %reshape.196 = bf16[4,1536,2,2,128]{4,3,2,1,0:T(2,128)(2,1)} reshape(bf16[48,128,512]{2,1,0:T(8,128)(2,1)} %gather_fusion) | data formatting | bytes 12582912 | tf_op jit(solution)/shard_map/while/body/eval_jaxpr/reshape | solution.py:79
  100.1 8.4 %fusion.65 = (bf16[4,1536,1,2,128]{4,3,2,1,0:T(2,128)(2,1)}, bf16[4,1536,1,2,128]{4,3,2,1,0:T(2,128)(2,1)}) fusion(bf16[4,1536,2,2,128]{4,3,2,1,0:T(2,128)(2,1)} %reshape.196), kind=kLoop, calls=%fused_computation.48.clone.1 | loop fusion | bytes 12582912 | tf_op jit(solution)/shard_map/while/body/eval_jaxpr/slice | solution.py:81
  108.5 6.9 %fusion.66 = (f32[4,2,128]{2,1,0:T(2,128)S(1)}, f32[4,2,128,1536]{3,2,1,0:T(8,128)}) fusion(pred[4,1536]{1,0:T(4,128)(4,1)S(1)} %bitcast.172, bf16[4,1536,1,2,128]{4,3,2,1,0:T(2,128)(2,1)} %get-tuple-element.207, bf16[2,4,128,2,128]{2,4,3,1,0:T(8,128)(2,1)} %get-tuple-element.234, s32[]{:T(128)S(6)} %copy.148), kind=kOutput, calls=%fused_computation.49.clone.1 | convolution fusion | flops 408946176 | bytes 9709572 | tf_op jit(solution)/shard_map/while/body/eval_jaxpr/sub | solution.py:89
  115.4 5.2 %fusion.67 = f32[4,128,2]{1,2,0:T(2,128)S(1)} fusion(bf16[4,1536,1,2,128]{4,3,2,1,0:T(2,128)(2,1)} %get-tuple-element.210, bf16[1,4,128,2,128]{4,2,3,1,0:T(8,128)(2,1)} %copy.141, f32[4,2,128,1536]{3,2,1,0:T(8,128)} %get-tuple-element.208, f32[4,2,128]{2,1,0:T(2,128)S(1)} %get-tuple-element.209), kind=kOutput, calls=%fused_computation.25.clone.1 | convolution fusion | flops 406191104 | bytes 9707520 | tf_op jit(solution)/shard_map/while/body/eval_jaxpr/ghtk,gkhd->gthd/dot_general | solution.py:92
  120.6 1.4 copy-done.12
  122.0 2.0 multiply_convert_fusion.2
  125.3 3.7 convolution_bitcast_fusion.4
  128.9 3.6 convolution_bitcast_fusion.5
  132.5 10.9 %pad_maximum_fusion.4 = f32[4,1536,4,128]{1,3,2,0:T(8,128)} fusion(f32[4,1536,2,128]{1,3,2,0:T(8,128)} %convolution_bitcast_fusion.4, f32[4,1536,2,128]{1,3,2,0:T(8,128)} %convolution_bitcast_fusion.5), kind=kLoop, calls=%fused_computation.3.clone.1 | loop fusion | flops 3145728 | bytes 25165824 | tf_op jit(solution)/shard_map/while/body/eval_jaxpr/concatenate | solution.py:111
  143.4 14.6 %copy.142 = f32[4,1536,4,128]{3,2,1,0:T(4,128)} copy(f32[4,1536,4,128]{1,3,2,0:T(8,128)} %pad_maximum_fusion.4) | data formatting | bytes 25165824 | tf_op jit(solution)/shard_map/while/body/eval_jaxpr/concatenate | solution.py:111
  158.0 15.1 %reshape.197 = f32[48,128,512]{2,1,0:T(8,128)} reshape(f32[4,1536,4,128]{3,2,1,0:T(4,128)} %copy.142) | data formatting | bytes 25165824 | tf_op jit(solution)/shard_map/while/body/eval_jaxpr/reshape | solution.py:111
  173.1 27.8 %scatter_fusion = f32[24,128,512]{2,1,0:T(8,128)} fusion(f32[24,128,512]{2,1,0:T(8,128)} %get-tuple-element.221, s32[48]{0:T(128)S(1)} %reshape.195, f32[48,128,512]{2,1,0:T(8,128)} %reshape.197), kind=kCustom, calls=%fused_computation.1.clone.1 | custom fusion | flops 3145728 | bytes 37748928 | tf_op jit(solution)/shard_map/while/body/eval_jaxpr/scatter-add | solution.py:114
  203.0 4.9 %gather_fusion = bf16[48,128,512]{2,1,0:T(8,128)(2,1)} fusion(bf16[24,128,512]{2,1,0:T(8,128)(2,1)S(1)} %get-tuple-element.235, s32[1024]{0:T(1024)S(1)} %pad_clamp_fusion.2), kind=kCustom, calls=%fused_computation.clone.1 | custom fusion | bytes 12583104 | tf_op jit(solution)/shard_map/while/body/eval_jaxpr/gather | solution.py:79
  207.9 9.7 %reshape.196 = bf16[4,1536,2,2,128]{4,3,2,1,0:T(2,128)(2,1)} reshape(bf16[48,128,512]{2,1,0:T(8,128)(2,1)} %gather_fusion) | data formatting | bytes 12582912 | tf_op jit(solution)/shard_map/while/body/eval_jaxpr/reshape | solution.py:79
  217.6 8.4 %fusion.65 = (bf16[4,1536,1,2,128]{4,3,2,1,0:T(2,128)(2,1)}, bf16[4,1536,1,2,128]{4,3,2,1,0:T(2,128)(2,1)}) fusion(bf16[4,1536,2,2,128]{4,3,2,1,0:T(2,128)(2,1)} %reshape.196), kind=kLoop, calls=%fused_computation.48.clone.1 | loop fusion | bytes 12582912 | tf_op jit(solution)/shard_map/while/body/eval_jaxpr/slice | solution.py:81
  226.0 6.9 %fusion.66 = (f32[4,2,128]{2,1,0:T(2,128)S(1)}, f32[4,2,128,1536]{3,2,1,0:T(8,128)}) fusion(pred[4,1536]{1,0:T(4,128)(4,1)S(1)} %bitcast.172, bf16[4,1536,1,2,128]{4,3,2,1,0:T(2,128)(2,1)} %get-tuple-element.207, bf16[2,4,128,2,128]{2,4,3,1,0:T(8,128)(2,1)} %get-tuple-element.234, s32[]{:T(128)S(6)} %copy.148), kind=kOutput, calls=%fused_computation.49.clone.1 | convolution fusion | flops 408946176 | bytes 9709572 | tf_op jit(solution)/shard_map/while/body/eval_jaxpr/sub | solution.py:89
  232.9 5.2 %fusion.67 = f32[4,128,2]{1,2,0:T(2,128)S(1)} fusion(bf16[4,1536,1,2,128]{4,3,2,1,0:T(2,128)(2,1)} %get-tuple-element.210, bf16[1,4,128,2,128]{4,2,3,1,0:T(8,128)(2,1)} %copy.141, f32[4,2,128,1536]{3,2,1,0:T(8,128)} %get-tuple-element.208, f32[4,2,128]{2,1,0:T(2,128)S(1)} %get-tuple-element.209), kind=kOutput, calls=%fused_computation.25.clone.1 | convolution fusion | flops 406191104 | bytes 9707520 | tf_op jit(solution)/shard_map/while/body/eval_jaxpr/ghtk,gkhd->gthd/dot_general | solution.py:92
  238.1 1.4 copy-done.12
  239.5 2.0 multiply_convert_fusion.2
  242.8 3.7 convolution_bitcast_fusion.4
  246.5 3.6 convolution_bitcast_fusion.5
  250.1 10.9 %pad_maximum_fusion.4 = f32[4,1536,4,128]{1,3,2,0:T(8,128)} fusion(f32[4,1536,2,128]{1,3,2,0:T(8,128)} %convolution_bitcast_fusion.4, f32[4,1536,2,128]{1,3,2,0:T(8,128)} %convolution_bitcast_fusion.5), kind=kLoop, calls=%fused_computation.3.clone.1 | loop fusion | flops 3145728 | bytes 25165824 | tf_op jit(solution)/shard_map/while/body/eval_jaxpr/concatenate | solution.py:111
  260.9 14.6 %copy.142 = f32[4,1536,4,128]{3,2,1,0:T(4,128)} copy(f32[4,1536,4,128]{1,3,2,0:T(8,128)} %pad_maximum_fusion.4) | data formatting | bytes 25165824 | tf_op jit(solution)/shard_map/while/body/eval_jaxpr/concatenate | solution.py:111
  275.5 15.1 %reshape.197 = f32[48,128,512]{2,1,0:T(8,128)} reshape(f32[4,1536,4,128]{3,2,1,0:T(4,128)} %copy.142) | data formatting | bytes 25165824 | tf_op jit(solution)/shard_map/while/body/eval_jaxpr/reshape | solution.py:111
  290.6 28.0 %scatter_fusion = f32[24,128,512]{2,1,0:T(8,128)} fusion(f32[24,128,512]{2,1,0:T(8,128)} %get-tuple-element.221, s32[48]{0:T(128)S(1)} %reshape.195, f32[48,128,512]{2,1,0:T(8,128)} %reshape.197), kind=kCustom, calls=%fused_computation.1.clone.1 | custom fusion | flops 3145728 | bytes 37748928 | tf_op jit(solution)/shard_map/while/body/eval_jaxpr/scatter-add | solution.py:114
  318.7 5.9 %fusion.41 = (f32[8,128,512]{2,1,0:T(8,128)S(1)}, f32[8,128,512]{2,1,0:T(8,128)}, f32[8,128,512]{2,1,0:T(8,128)}) fusion(f32[24,128,512]{2,1,0:T(8,128)} %get-tuple-element.87), kind=kLoop, calls=%fused_computation.50 | loop fusion | bytes 12582912 | tf_op jit(solution)/shard_map/slice | solution.py:40
  325.9 5.7 %collective-permute-start.2 = (f32[1024,512]{1,0:T(8,128)}, f32[1024,512]{1,0:T(8,128)}, u32[]{:S(2)}, u32[]{:S(2)}) collective-permute-start(f32[1024,512]{1,0:T(8,128)} %bitcast.30), channel_id=1, source_target_pairs={{0,1},{2,3},{4,5},{6,7},{8,9},{10,11},{12,13},{14,15},{16,17},{18,... | collective-permute-start | bytes 6291464 | tf_op jit(solution)/shard_map/ppermute | solution.py:23
  332.6 3.6 all-to-all-start.4
  336.2 2.9 fusion.36
  340.1 9.0 %all-to-all-done.4 = bf16[8,128,256]{2,1,0:T(8,128)(2,1)S(1)} async-done(((bf16[8,128,256]{2,1,0:T(8,128)(2,1)}), bf16[8,128,256]{2,1,0:T(8,128)(2,1)S(1)}, u32[]{:S(2)}, u32[]{:S(2)}) %all-to-all-start.4) | async-done | bytes 524320 | tf_op jit(solution)/shard_map/all_to_all | solution.py:123
  349.0 17.2 %all_to_all.118 = bf16[8,128,256]{2,1,0:T(8,128)(2,1)S(1)} all-to-all(bf16[8,128,256]{2,1,0:T(8,128)(2,1)S(1)} %bitcast.170), channel_id=1, replica_groups=mesh['groups'=2,'seq'=8,'tensor'=2] {'seq'}, dimensions={0} | all-to-all | bytes 1048576 | tf_op jit(solution)/shard_map/all_to_all | solution.py:126
  366.2 3.6 all-to-all-start.6
  372.4 11.5 %all-to-all-done.6 = bf16[8,128,256]{2,1,0:T(8,128)(2,1)S(1)} async-done(((bf16[8,128,256]{2,1,0:T(8,128)(2,1)}), bf16[8,128,256]{2,1,0:T(8,128)(2,1)S(1)}, u32[]{:S(2)}, u32[]{:S(2)}) %all-to-all-start.6) | async-done | bytes 524320 | tf_op jit(solution)/shard_map/all_to_all | solution.py:127
  (74 shorter events, 19.0 us)
Async XLA Ops:
  0.6 27.8 %copy-start.6 = (bf16[1,128,2048]{2,1,0:T(8,128)(2,1)S(1)}, bf16[1,128,2048]{2,1,0:T(8,128)(2,1)}, u32[]{:S(2)}) copy-start(bf16[1,128,2048]{2,1,0:T(8,128)(2,1)} %param.15) | copy-start | bytes 1572868
  0.6 52.5 %copy-start.7 = (bf16[1,128,2048]{2,1,0:T(8,128)(2,1)S(1)}, bf16[1,128,2048]{2,1,0:T(8,128)(2,1)}, u32[]{:S(2)}) copy-start(bf16[1,128,2048]{2,1,0:T(8,128)(2,1)} %param.18) | copy-start | bytes 1572868
  3.1 21.8 %all-to-all-start.1 = ((bf16[128,8,256]{2,0,1:T(8,128)(2,1)}), bf16[128,8,256]{2,0,1:T(8,128)(2,1)S(1)}, u32[]{:S(2)}, u32[]{:S(2)}) async-start(bf16[128,8,256]{2,0,1:T(8,128)(2,1)} %copy.77), calls=%async_computation.1 | async-start | bytes 1048576 | tf_op jit(solution)/shard_map/all_to_all | solution.py:60
  24.8 40.8 %copy-start.4 = (bf16[128,8,256]{2,0,1:T(8,128)(2,1)}, bf16[128,8,256]{2,0,1:T(8,128)(2,1)S(1)}, u32[]{:S(2)}) copy-start(bf16[128,8,256]{2,0,1:T(8,128)(2,1)S(1)} %all-to-all-done.1) | copy-start | bytes 1572868
  24.8 18.3 %all-to-all-start.2 = ((bf16[128,8,256]{2,0,1:T(8,128)(2,1)}), bf16[128,8,256]{2,0,1:T(8,128)(2,1)S(1)}, u32[]{:S(2)}, u32[]{:S(2)}) async-start(bf16[128,8,256]{2,0,1:T(8,128)(2,1)} %copy.79), calls=%async_computation.2 | async-start | bytes 1048576 | tf_op jit(solution)/shard_map/all_to_all | solution.py:61
  43.1 22.5 %copy-start.5 = (bf16[128,8,256]{2,0,1:T(8,128)(2,1)}, bf16[128,8,256]{2,0,1:T(8,128)(2,1)S(1)}, u32[]{:S(2)}) copy-start(bf16[128,8,256]{2,0,1:T(8,128)(2,1)S(1)} %all-to-all-done.2) | copy-start | bytes 1572868
  43.1 18.3 %all-to-all-start = ((bf16[128,8,256]{0,2,1:T(8,128)(2,1)}), bf16[128,8,256]{0,2,1:T(8,128)(2,1)S(1)}, u32[]{:S(2)}, u32[]{:S(2)}) async-start(bf16[128,8,256]{0,2,1:T(8,128)(2,1)} %bitcast.13), calls=%async_computation | async-start | bytes 1048576 | tf_op jit(solution)/shard_map/all_to_all | solution.py:59
  46.9 18.8 %collective-permute-start.1 = (bf16[1024,512]{1,0:T(8,128)(2,1)S(1)}, bf16[1024,512]{1,0:T(8,128)(2,1)}, u32[]{:S(2)}, u32[]{:S(2)}) collective-permute-start(bf16[1024,512]{1,0:T(8,128)(2,1)S(1)} %pad_maximum_fusion.2), channel_id=1, source_target_pairs={{1,0},{3,2},{5,4},{7,6},{9,8},{11,10},{13,12},{15,14},{17,16},{19,... | collective-permute-start | bytes 3145736 | tf_op jit(solution)/shard_map/ppermute | solution.py:26
  48.2 17.5 %collective-permute-start = (bf16[1024,512]{1,0:T(8,128)(2,1)S(1)}, bf16[1024,512]{1,0:T(8,128)(2,1)}, u32[]{:S(2)}, u32[]{:S(2)}) collective-permute-start(bf16[1024,512]{1,0:T(8,128)(2,1)S(1)} %pad_maximum_fusion.2), channel_id=1, source_target_pairs={{0,1},{2,3},{4,5},{6,7},{8,9},{10,11},{12,13},{14,15},{16,17},{18,... | collective-permute-start | bytes 3145736 | tf_op jit(solution)/shard_map/ppermute | solution.py:23
  61.5 4.2 %copy-start.2 = (bf16[128,8,256]{0,2,1:T(8,128)(2,1)}, bf16[128,8,256]{0,2,1:T(8,128)(2,1)S(1)}, u32[]{:S(2)}) copy-start(bf16[128,8,256]{0,2,1:T(8,128)(2,1)S(1)} %all-to-all-done) | copy-start | bytes 1572868
  61.5 18.4 %all-to-all-start.3 = ((bf16[128,8,256]{0,2,1:T(8,128)(2,1)}), bf16[128,8,256]{0,2,1:T(8,128)(2,1)}, u32[]{:S(2)}, u32[]{:S(2)}) async-start(bf16[128,8,256]{0,2,1:T(8,128)(2,1)} %bitcast.23), calls=%async_computation.3 | async-start | bytes 1048576 | tf_op jit(solution)/shard_map/all_to_all | solution.py:62
  65.6 17.8 %copy-start.11 = (s32[8,12]{1,0:T(8,128)S(1)}, s32[8,12]{1,0:T(8,128)}, u32[]{:S(2)}) copy-start(s32[8,12]{1,0:T(8,128)} %param.19) | copy-start | bytes 1156
  115.4 5.2 %copy-start.1 = (bf16[4,1536,1,2,128]{4,3,2,1,0:T(2,128)(2,1)S(1)}, bf16[4,1536,1,2,128]{4,3,2,1,0:T(2,128)(2,1)}, u32[]{:S(2)}) copy-start(bf16[4,1536,1,2,128]{4,3,2,1,0:T(2,128)(2,1)} %get-tuple-element.210) | copy-start | bytes 9437188 | tf_op jit(solution)/shard_map/while
  115.4 6.6 %copy-start.12 = (f32[4,2,128,1536]{3,2,1,0:T(8,128)S(1)}, f32[4,2,128,1536]{3,2,1,0:T(8,128)}, u32[]{:S(2)}) copy-start(f32[4,2,128,1536]{3,2,1,0:T(8,128)} %get-tuple-element.208) | copy-start | bytes 18874372 | tf_op jit(solution)/shard_map/while
  122.0 2.0 copy-start
  122.0 2.0 copy-start.8
  125.3 3.7 copy-start.9
  125.3 3.7 copy-start.3
  232.9 5.2 %copy-start.1 = (bf16[4,1536,1,2,128]{4,3,2,1,0:T(2,128)(2,1)S(1)}, bf16[4,1536,1,2,128]{4,3,2,1,0:T(2,128)(2,1)}, u32[]{:S(2)}) copy-start(bf16[4,1536,1,2,128]{4,3,2,1,0:T(2,128)(2,1)} %get-tuple-element.210) | copy-start | bytes 9437188 | tf_op jit(solution)/shard_map/while
  232.9 6.6 %copy-start.12 = (f32[4,2,128,1536]{3,2,1,0:T(8,128)S(1)}, f32[4,2,128,1536]{3,2,1,0:T(8,128)}, u32[]{:S(2)}) copy-start(f32[4,2,128,1536]{3,2,1,0:T(8,128)} %get-tuple-element.208) | copy-start | bytes 18874372 | tf_op jit(solution)/shard_map/while
  239.5 2.0 copy-start
  239.5 2.0 copy-start.8
  242.8 3.7 copy-start.9
  242.8 3.7 copy-start.3
  318.7 12.9 %copy-start.10 = (bf16[2,4,128,2,128]{2,4,3,1,0:T(8,128)(2,1)S(1)}, bf16[2,4,128,2,128]{2,4,3,1,0:T(8,128)(2,1)}, u32[]{:S(2)}) copy-start(bf16[2,4,128,2,128]{2,4,3,1,0:T(8,128)(2,1)} %get-tuple-element.86) | copy-start | bytes 1572868
  324.6 11.7 %collective-permute-start.3 = (f32[1024,512]{1,0:T(8,128)}, f32[1024,512]{1,0:T(8,128)}, u32[]{:S(2)}, u32[]{:S(2)}) collective-permute-start(f32[1024,512]{1,0:T(8,128)} %bitcast.31), channel_id=1, source_target_pairs={{1,0},{3,2},{5,4},{7,6},{9,8},{11,10},{13,12},{15,14},{17,16},{19,... | collective-permute-start | bytes 6291464 | tf_op jit(solution)/shard_map/ppermute | solution.py:26
  325.9 10.4 %collective-permute-start.2 = (f32[1024,512]{1,0:T(8,128)}, f32[1024,512]{1,0:T(8,128)}, u32[]{:S(2)}, u32[]{:S(2)}) collective-permute-start(f32[1024,512]{1,0:T(8,128)} %bitcast.30), channel_id=1, source_target_pairs={{0,1},{2,3},{4,5},{6,7},{8,9},{10,11},{12,13},{14,15},{16,17},{18,... | collective-permute-start | bytes 6291464 | tf_op jit(solution)/shard_map/ppermute | solution.py:23
  332.6 16.4 %all-to-all-start.4 = ((bf16[8,128,256]{2,1,0:T(8,128)(2,1)}), bf16[8,128,256]{2,1,0:T(8,128)(2,1)S(1)}, u32[]{:S(2)}, u32[]{:S(2)}) async-start(bf16[8,128,256]{2,1,0:T(8,128)(2,1)} %copy.95), calls=%async_computation.4 | async-start | bytes 1048576 | tf_op jit(solution)/shard_map/all_to_all | solution.py:123
  366.2 17.7 %all-to-all-start.6 = ((bf16[8,128,256]{2,1,0:T(8,128)(2,1)}), bf16[8,128,256]{2,1,0:T(8,128)(2,1)S(1)}, u32[]{:S(2)}, u32[]{:S(2)}) async-start(bf16[8,128,256]{2,1,0:T(8,128)(2,1)} %bitcast.35), calls=%async_computation.6 | async-start | bytes 1048576 | tf_op jit(solution)/shard_map/all_to_all | solution.py:127
where the time goes:
time: 388 us; the launch traced here: 385 us
  local copies, waits for them, and re-layouts  134 us (35%)
  other arithmetic  82.7 us (21%)
  waiting for transfers between devices  65.6 us (17%)
  matrix products  45.2 us (12%)
  starting transfers between devices  39.3 us (10%)
  blocking collectives  17.2 us (4%)
    scatter-add x2, other arithmetic, attend_block(): totals = totals.at[local_tile].add(key_terms)  55.9 us
    reshape x2, local copies, waits for them, and re-layouts, attend_block(): jnp.concatenate([key_part, value_part], 2)  30.2 us
    concatenate x2, local copies, waits for them, and re-layouts, attend_block(): jnp.concatenate([key_part, value_part], 2)  29.2 us
    concatenate x2, other arithmetic, attend_block(): jnp.concatenate([key_part, value_part], 2)  21.7 us
    reshape x2, local copies, waits for them, and re-layouts, attend_block(): kv_tiles[local_tile].reshape(block_tiles, WIN * TILE, 2, heads_here, DH)  19.4 us
    all_to_all x1, blocking collectives, body(): lax.all_to_all(key_grad, 'seq', split_axis=0, concat_axis=1, tiled=True)  17.2 us
    slice x2, local copies, waits for them, and re-layouts, attend_block(): value_sel = picked[:, :, 1]  16.9 us
    sub x2, matrix products, attend_block(): weights = jnp.exp(scores - row_max)  13.8 us
  transfers between devices with their start and end apart: 10, of which 6 were waited for; matrix products, arithmetic and copies ran while one was open for 4% of the time, Pallas kernels for 0%

commit v1 on v0

--- a/solution.py
+++ b/solution.py
@@ -1,8 +1,11 @@
+import functools
 import math
 
 import jax
 import jax.numpy as jnp
 from jax import lax
+from jax.experimental import pallas as pl
+from jax.experimental.pallas import tpu as pltpu
 from jax.sharding import PartitionSpec as P
 
 HEADS = 16
@@ -44,7 +47,7 @@
     return (own_rows[:, :local_width], own_rows[:, local_width:])
 
 
-def body(queries, keys, values, out_grad, tile_lists):
+def regrouped_body(queries, keys, values, out_grad, tile_lists):
     span_rows = queries.shape[1]
     feature_count = queries.shape[2]
     seq_count = lax.axis_size("seq")
@@ -134,6 +137,347 @@
     )
 
 
+def partner_order(seq_count, tensor_count):
+    order = []
+    for step in range(seq_count):
+        reach = (seq_count // 2 + ((step + 1) // 2) * (2 * (step % 2) - 1)) % seq_count
+        for turn in range(tensor_count):
+            if reach or turn:
+                order.append((reach, turn))
+    return order
+
+
+def head_kernel(
+    seq_count,
+    tensor_count,
+    q_hbm,
+    k_hbm,
+    v_hbm,
+    g_hbm,
+    lists_hbm,
+    dq_hbm,
+    dk_hbm,
+    dv_hbm,
+    q_all,
+    k_all,
+    v_all,
+    g_all,
+    lists_all,
+    bias,
+    probs,
+    prob_grad,
+    key_t,
+    dv_sum,
+    dk_sum,
+    dq_out,
+    dk_out,
+    dv_out,
+    in_send,
+    in_recv,
+    out_send,
+    out_recv,
+    list_send,
+    list_recv,
+    local_sem,
+):
+    seq_here = lax.axis_index("seq")
+    tensor_here = lax.axis_index("tensor")
+    me = tensor_here * seq_count + seq_here
+    tiles = seq_count * tensor_count
+    pairs = tiles // 2
+    score_scale = 1.0 / math.sqrt(DH)
+    partners = []
+    for reach, turn in partner_order(seq_count, tensor_count):
+        seq_there = lax.rem(seq_here + reach, seq_count)
+        tensor_there = lax.rem(tensor_here + turn, tensor_count)
+        partners.append((seq_there, tensor_there, tensor_there * seq_count + seq_there))
+
+    def columns(index):
+        return pl.ds(pl.multiple_of(index * DH, DH), DH)
+
+    def remote(src, dst, send, recv, seq_there, tensor_there):
+        return pltpu.make_async_remote_copy(
+            src_ref=src,
+            dst_ref=dst,
+            send_sem=send,
+            recv_sem=recv,
+            device_id={"seq": seq_there, "tensor": tensor_there},
+            device_id_type=pl.DeviceIdType.MESH,
+        )
+
+    incoming = ((q_hbm, q_all), (k_hbm, k_all), (g_hbm, g_all), (v_hbm, v_all))
+    outgoing = ((dv_out, dv_hbm), (dq_out, dq_hbm), (dk_out, dk_hbm))
+
+    def in_copy(which, seq_there, tensor_there, there):
+        src, dst = incoming[which]
+        return remote(
+            src.at[:, columns(there)],
+            dst.at[me],
+            in_send.at[which, there],
+            in_recv.at[which, me],
+            seq_there,
+            tensor_there,
+        )
+
+    def in_wait(which, seq_there, tensor_there, there):
+        src, dst = incoming[which]
+        remote(
+            src.at[:, columns(there)],
+            dst.at[there],
+            in_send.at[which, there],
+            in_recv.at[which, there],
+            seq_there,
+            tensor_there,
+        ).wait()
+
+    def in_local(which):
+        src, dst = incoming[which]
+        return pltpu.make_async_copy(src.at[:, columns(me)], dst.at[me], local_sem.at[which])
+
+    def out_copy(which, seq_there, tensor_there, there):
+        src, dst = outgoing[which]
+        return remote(
+            src.at[there],
+            dst.at[:, columns(me)],
+            out_send.at[which, there],
+            out_recv.at[which, me],
+            seq_there,
+            tensor_there,
+        )
+
+    def out_wait(which, seq_there, tensor_there, there):
+        src, dst = outgoing[which]
+        remote(
+            src.at[there],
+            dst.at[:, columns(there)],
+            out_send.at[which, there],
+            out_recv.at[which, there],
+            seq_there,
+            tensor_there,
+        ).wait()
+
+    def out_local(which):
+        src, dst = outgoing[which]
+        return pltpu.make_async_copy(src.at[me], dst.at[:, columns(me)], local_sem.at[4 + which])
+
+    for which in range(4):
+        in_local(which).start()
+    own_list = pltpu.make_async_copy(lists_hbm, lists_all.at[tensor_here], local_sem.at[7])
+    own_list.start()
+
+    barrier = pltpu.get_barrier_semaphore()
+    for seq_there, tensor_there, _ in partners:
+        pl.semaphore_signal(
+            barrier,
+            inc=1,
+            device_id={"seq": seq_there, "tensor": tensor_there},
+            device_id_type=pl.DeviceIdType.MESH,
+        )
+    pl.semaphore_wait(barrier, len(partners))
+
+    def list_copy(turn, slot):
+        return remote(
+            lists_hbm,
+            lists_all.at[slot],
+            list_send.at[turn],
+            list_recv.at[slot],
+            seq_here,
+            lax.rem(tensor_here + turn, tensor_count),
+        )
+
+    for turn in range(1, tensor_count):
+        list_copy(turn, tensor_here).start()
+    for group in ((0, 1), (2,), (3,)):
+        for partner in partners:
+            for which in group:
+                in_copy(which, *partner).start()
+
+    own_list.wait()
+    for turn in range(1, tensor_count):
+        list_copy(turn, lax.rem(tensor_here + turn, tensor_count)).wait()
+    tile_ids = lax.broadcasted_iota(jnp.int32, (tiles, TILE), 0)
+    for tile in range(tiles):
+        row = lists_all[tile // seq_count, tile % seq_count : tile % seq_count + 1, :]
+        miss = jnp.full((tiles, TILE), -1e30, jnp.float32)
+        for entry in range(WIN):
+            miss = jnp.where(row[:, entry : entry + 1] == tile_ids, 0.0, miss)
+        half = (tile % 2) * TILE
+        bias[tile // 2, :, half : half + TILE] = miss
+
+    dv_sum[...] = jnp.zeros_like(dv_sum)
+    dk_sum[...] = jnp.zeros_like(dk_sum)
+
+    for which in (0, 1):
+        in_local(which).wait()
+    for partner in partners:
+        for which in (0, 1):
+            in_wait(which, *partner)
+
+    def pair_rows(ref, index):
+        return ref[pl.ds(2 * index, 2)].reshape(2 * TILE, DH)
+
+    def turned(block):
+        return block.astype(jnp.float32).T.astype(jnp.bfloat16)
+
+    def key_rows(index):
+        return pl.ds(index * 2 * TILE, 2 * TILE)
+
+    def fold(block, op):
+        return op(block.reshape(2 * TILE // 8, 8, 2 * TILE), axis=0)
+
+    def score_pair(pair, _):
+        query_t = turned(pair_rows(q_all, pair))
+        key_t[pair] = turned(pair_rows(k_all, pair))
+        top = jnp.full((8, 2 * TILE), -3e38, jnp.float32)
+        for chunk in range(pairs):
+            scores = (
+                jnp.dot(pair_rows(k_all, chunk), query_t, preferred_element_type=jnp.float32)
+                * score_scale
+            )
+            scores = jnp.concatenate(
+                [
+                    scores[:TILE] + bias[pair, 2 * chunk : 2 * chunk + 1, :],
+                    scores[TILE:] + bias[pair, 2 * chunk + 1 : 2 * chunk + 2, :],
+                ],
+                axis=0,
+            )
+            probs[pair, key_rows(chunk), :] = scores
+            top = jnp.maximum(top, fold(scores, jnp.max))
+        top = jnp.max(top, axis=0, keepdims=True)
+        total = jnp.zeros((8, 2 * TILE), jnp.float32)
+        for chunk in range(pairs):
+            weights = jnp.exp(probs[pair, key_rows(chunk), :] - top)
+            probs[pair, key_rows(chunk), :] = weights
+            total = total + fold(weights, jnp.sum)
+        inverse = 1.0 / jnp.sum(total, axis=0, keepdims=True)
+        for chunk in range(pairs):
+            probs[pair, key_rows(chunk), :] = probs[pair, key_rows(chunk), :] * inverse
+        return 0
+
+    lax.fori_loop(0, pairs, score_pair, 0)
+
+    in_local(2).wait()
+    for partner in partners:
+        in_wait(2, *partner)
+
+    def value_pair(pair, _):
+        grad_pair = pair_rows(g_all, pair)
+        for chunk in range(pairs):
+            dv_sum[key_rows(chunk), :] += jnp.dot(
+                probs[pair, key_rows(chunk), :].astype(jnp.bfloat16),
+                grad_pair,
+                preferred_element_type=jnp.float32,
+            )
+        return 0
+
+    lax.fori_loop(0, pairs, value_pair, 0)
+    dv_out[...] = dv_sum[...].astype(jnp.bfloat16).reshape(dv_out.shape)
+    for partner in partners:
+        out_copy(0, *partner).start()
+    out_local(0).start()
+
+    in_local(3).wait()
+    for partner in partners:
+        in_wait(3, *partner)
+
+    def grad_pair_step(pair, _):
+        query_pair = pair_rows(q_all, pair)
+        grad_t = turned(pair_rows(g_all, pair))
+        delta = jnp.zeros((8, 2 * TILE), jnp.float32)
+        for chunk in range(pairs):
+            product = jnp.dot(pair_rows(v_all, chunk), grad_t, preferred_element_type=jnp.float32)
+            prob_grad[key_rows(chunk), :] = product
+            rounded = probs[pair, key_rows(chunk), :].astype(jnp.bfloat16).astype(jnp.float32)
+            delta = delta + fold(rounded * product, jnp.sum)
+        delta = jnp.sum(delta, axis=0, keepdims=True)
+        query_sum = jnp.zeros((DH, 2 * TILE), jnp.float32)
+        for chunk in range(pairs):
+            score_grad = (
+                probs[pair, key_rows(chunk), :]
+                * (prob_grad[key_rows(chunk), :] - delta)
+                * score_scale
+            ).astype(jnp.bfloat16)
+            dk_sum[key_rows(chunk), :] += jnp.dot(
+                score_grad, query_pair, preferred_element_type=jnp.float32
+            )
+            query_sum = query_sum + jnp.dot(
+                key_t[chunk], score_grad, preferred_element_type=jnp.float32
+            )
+        dq_out[pl.ds(2 * pair, 2)] = query_sum.T.astype(jnp.bfloat16).reshape(2, TILE, DH)
+        for side in range(2):
+            there = 2 * pair + side
+
+            @pl.when(there != me)
+            def _():
+                out_copy(1, lax.rem(there, seq_count), there // seq_count, there).start()
+
+        return 0
+
+    lax.fori_loop(0, pairs, grad_pair_step, 0)
+    dk_out[...] = dk_sum[...].astype(jnp.bfloat16).reshape(dk_out.shape)
+    for partner in partners:
+        out_copy(2, *partner).start()
+    out_local(1).start()
+    out_local(2).start()
+
+    for which in range(3):
+        out_local(which).wait()
+        for partner in partners:
+            out_wait(which, *partner)
+
+
+def head_body(queries, keys, values, out_grad, tile_lists):
+    seq_count = lax.axis_size("seq")
+    tensor_count = lax.axis_size("tensor")
+    tiles = seq_count * tensor_count
+    pairs = tiles // 2
+    shape = (TILE, HEADS * DH)
+    blocks = [array.reshape(shape) for array in (queries, keys, values, out_grad)]
+    anywhere = pl.BlockSpec(memory_space=pl.ANY)
+    per_tile = pltpu.VMEM((tiles, TILE, DH), jnp.bfloat16)
+    grads = pl.pallas_call(
+        functools.partial(head_kernel, seq_count, tensor_count),
+        out_shape=[jax.ShapeDtypeStruct(shape, jnp.bfloat16)] * 3,
+        in_specs=[anywhere] * 5,
+        out_specs=[anywhere] * 3,
+        scratch_shapes=[
+            per_tile,
+            per_tile,
+            per_tile,
+            per_tile,
+            pltpu.VMEM((tensor_count,) + tile_lists.shape, jnp.int32),
+            pltpu.VMEM((pairs, tiles, 2 * TILE), jnp.float32),
+            pltpu.VMEM((pairs, tiles * TILE, 2 * TILE), jnp.float32),
+            pltpu.VMEM((tiles * TILE, 2 * TILE), jnp.float32),
+            pltpu.VMEM((pairs, DH, 2 * TILE), jnp.bfloat16),
+            pltpu.VMEM((tiles * TILE, DH), jnp.float32),
+            pltpu.VMEM((tiles * TILE, DH), jnp.float32),
+            per_tile,
+            per_tile,
+            per_tile,
+            pltpu.SemaphoreType.DMA((4, tiles)),
+            pltpu.SemaphoreType.DMA((4, tiles)),
+            pltpu.SemaphoreType.DMA((3, tiles)),
+            pltpu.SemaphoreType.DMA((3, tiles)),
+            pltpu.SemaphoreType.DMA((tensor_count,)),
+            pltpu.SemaphoreType.DMA((tensor_count,)),
+            pltpu.SemaphoreType.DMA((8,)),
+        ],
+        compiler_params=pltpu.CompilerParams(
+            collective_id=0, has_side_effects=True, vmem_limit_bytes=60 * 1024 * 1024
+        ),
+    )(*blocks, tile_lists)
+    return tuple(grad.reshape(queries.shape) for grad in grads)
+
+
+def body(queries, keys, values, out_grad, tile_lists):
+    devices = lax.axis_size("seq") * lax.axis_size("tensor")
+    one_head_one_tile = devices == HEADS and queries.shape[:2] == (1, TILE)
+    if one_head_one_tile and queries.shape[2] == HEADS * DH:
+        return head_body(queries, keys, values, out_grad, tile_lists)
+    return regrouped_body(queries, keys, values, out_grad, tile_lists)
+
+
 def solution(mesh):
     return jax.shard_map(
         body,

time: 388 us -> 92.2 us (0.24)
  local copies, waits for them, and re-layouts: 134 us -> 3.97 us
  Pallas kernels: 0 us -> 87.3 us
  other arithmetic: 82.7 us -> 0 us
  waiting for transfers between devices: 65.6 us -> 0 us
  matrix products: 45.2 us -> 0 us
  starting transfers between devices: 39.3 us -> 0 us
  blocking collectives: 17.2 us -> 0 us
    pallas_call x0 -> x1, Pallas kernels: none -> 87.3 us  [head_body(): pl.pallas_call(functools.partial(head_kernel, seq_count, tensor_count), o...]
    all_to_all x6 -> x0, waiting for transfers between devices: 65.6 us -> none  [the longest x1 13.7 us: body(): lax.all_to_all(value_tokens, 'seq', split_axis=1, concat_axis=0, tiled=True)]
    scatter-add x2 -> x0, other arithmetic: 55.9 us -> none  [attend_block(): totals = totals.at[local_tile].add(key_terms)]
    reshape x4 -> x0, local copies, waits for them, and re-layouts: 49.6 us -> none  [the longest x2 30.2 us: attend_block(): jnp.concatenate([key_part, value_part], 2)]
    dot_general x10 -> x0, matrix products: 31.4 us -> none  [the longest x2 10.4 us: attend_block(): jnp.einsum('ghtk,gkhd->gthd', weights_b, value_sel, preferred_element_typ...]
    concatenate x2 -> x0, local copies, waits for them, and re-layouts: 29.2 us -> none  [attend_block(): jnp.concatenate([key_part, value_part], 2)]
    all_to_all x6 -> x0, starting transfers between devices: 26 us -> none  [the longest x1 7.28 us: body(): lax.all_to_all(key_tokens, 'seq', split_axis=1, concat_axis=0, tiled=True)]
    concatenate x4 -> x0, other arithmetic: 23.9 us -> none  [the longest x2 21.7 us: attend_block(): jnp.concatenate([key_part, value_part], 2)]
  transfers between devices with their start and end apart: 10 -> 0, of which waited for: 6 -> 0; matrix products, arithmetic and copies ran while one was open for 4% -> 0% of each run, Pallas kernels for 0% -> 0%
where the time goes in v1:
time: 92.2 us; the launch traced here: 92 us
  Pallas kernels  87.3 us (95%)
  local copies, waits for them, and re-layouts  3.97 us (4%)
    pallas_call x1, Pallas kernels, head_body(): pl.pallas_call(functools.partial(head_kernel, seq_count, tensor_count), o...  87.3 us
    unnamed x7, local copies, waits for them, and re-layouts  3.97 us

profile of v1, /device:TPU:0, one launch (start us, length us, event | category | flops | bytes accessed | tf_op | source)
XLA Modules:
  0.0 92.0 jit_solution(14942089426126877397)
XLA Ops:
  0.6 87.3 %shard_map.76 = (bf16[128,2048]{1,0:T(8,128)(2,1)}, bf16[128,2048]{1,0:T(8,128)(2,1)}, bf16[128,2048]{1,0:T(8,128)(2,1)}) custom-call(bf16[128,2048]{1,0:T(8,128)(2,1)} %bitcast.10, bf16[128,2048]{1,0:T(8,128)(2,1)} %bitcast.11, bf16[128,2048]{1,0:T(8,128)(2,1)} %bitcast.12, bf16[128,2048]{1,0:T(8,128)(2,1)} %bitcast.13, s32[8,12]{1,0:T(8,128)} %lists_hbm.1), custom_call_target="tpu_custom_call" | custom-call | tf_op jit(solution)/shard_map/pallas_call | solution.py:438
  88.0 0.0 copy-start.1
  88.0 1.9 %copy.11 = bf16[1,128,2048]{2,1,0:T(8,128)(2,1)} copy(bf16[1,128,2048]{2,1,0:T(8,128)(2,1)} %bitcast.9) | data formatting | bytes 1048576
  89.9 0.0 copy-done.1
  89.9 0.0 copy-start
  89.9 0.8 copy.12
  90.7 0.4 copy-done
  91.2 0.8 copy.13
Async XLA Ops:
  88.0 2.0 %copy-start.1 = (bf16[128,2048]{1,0:T(8,128)(2,1)S(1)}, bf16[128,2048]{1,0:T(8,128)(2,1)}, u32[]{:S(2)}) copy-start(bf16[128,2048]{1,0:T(8,128)(2,1)} %get-tuple-element.7) | copy-start | bytes 1572868
  89.9 1.2 %copy-start = (bf16[128,2048]{1,0:T(8,128)(2,1)S(1)}, bf16[128,2048]{1,0:T(8,128)(2,1)}, u32[]{:S(2)}) copy-start(bf16[128,2048]{1,0:T(8,128)(2,1)} %get-tuple-element.8) | copy-start | bytes 1572868

commit v2 on v1

--- a/solution.py
+++ b/solution.py
@@ -172,6 +172,7 @@
     dq_out,
     dk_out,
     dv_out,
+    staged,
     in_send,
     in_recv,
     out_send,
@@ -205,7 +206,13 @@
             device_id_type=pl.DeviceIdType.MESH,
         )
 
-    incoming = ((q_hbm, q_all), (k_hbm, k_all), (g_hbm, g_all), (v_hbm, v_all))
+    staging = [
+        pltpu.make_async_copy(src, staged.at[which], local_sem.at[8 + which])
+        for which, src in enumerate((q_hbm, k_hbm, g_hbm, v_hbm))
+    ]
+    incoming = tuple(
+        (staged.at[which], dst) for which, dst in enumerate((q_all, k_all, g_all, v_all))
+    )
     outgoing = ((dv_out, dv_hbm), (dq_out, dq_hbm), (dk_out, dk_hbm))
 
     def in_copy(which, seq_there, tensor_there, there):
@@ -260,8 +267,8 @@
         src, dst = outgoing[which]
         return pltpu.make_async_copy(src.at[me], dst.at[:, columns(me)], local_sem.at[4 + which])
 
-    for which in range(4):
-        in_local(which).start()
+    for copy in staging:
+        copy.start()
     own_list = pltpu.make_async_copy(lists_hbm, lists_all.at[tensor_here], local_sem.at[7])
     own_list.start()
 
@@ -288,6 +295,9 @@
     for turn in range(1, tensor_count):
         list_copy(turn, tensor_here).start()
     for group in ((0, 1), (2,), (3,)):
+        for which in group:
+            staging[which].wait()
+            in_local(which).start()
         for partner in partners:
             for which in group:
                 in_copy(which, *partner).start()
@@ -426,6 +436,28 @@
             out_wait(which, *partner)
 
 
+def settle_kernel(*refs):
+    copies = [
+        pltpu.make_async_copy(src, dst, refs[6].at[i])
+        for i, (src, dst) in enumerate(zip(refs[:3], refs[3:6]))
+    ]
+    for copy in copies:
+        copy.start()
+    for copy in copies:
+        copy.wait()
+
+
+def settle(grads):
+    anywhere = pl.BlockSpec(memory_space=pl.ANY)
+    return pl.pallas_call(
+        settle_kernel,
+        out_shape=[pltpu.HBM(grad.shape, grad.dtype) for grad in grads],
+        in_specs=[anywhere] * 3,
+        out_specs=[anywhere] * 3,
+        scratch_shapes=[pltpu.SemaphoreType.DMA((3,))],
+    )(*[pltpu.with_memory_space_constraint(grad, pltpu.VMEM) for grad in grads])
+
+
 def head_body(queries, keys, values, out_grad, tile_lists):
     seq_count = lax.axis_size("seq")
     tensor_count = lax.axis_size("tensor")
@@ -437,7 +469,7 @@
     per_tile = pltpu.VMEM((tiles, TILE, DH), jnp.bfloat16)
     grads = pl.pallas_call(
         functools.partial(head_kernel, seq_count, tensor_count),
-        out_shape=[jax.ShapeDtypeStruct(shape, jnp.bfloat16)] * 3,
+        out_shape=[pltpu.VMEM(shape, jnp.bfloat16)] * 3,
         in_specs=[anywhere] * 5,
         out_specs=[anywhere] * 3,
         scratch_shapes=[
@@ -455,19 +487,20 @@
             per_tile,
             per_tile,
             per_tile,
+            pltpu.VMEM((4,) + shape, jnp.bfloat16),
             pltpu.SemaphoreType.DMA((4, tiles)),
             pltpu.SemaphoreType.DMA((4, tiles)),
             pltpu.SemaphoreType.DMA((3, tiles)),
             pltpu.SemaphoreType.DMA((3, tiles)),
             pltpu.SemaphoreType.DMA((tensor_count,)),
             pltpu.SemaphoreType.DMA((tensor_count,)),
-            pltpu.SemaphoreType.DMA((8,)),
+            pltpu.SemaphoreType.DMA((12,)),
         ],
         compiler_params=pltpu.CompilerParams(
             collective_id=0, has_side_effects=True, vmem_limit_bytes=60 * 1024 * 1024
         ),
     )(*blocks, tile_lists)
-    return tuple(grad.reshape(queries.shape) for grad in grads)
+    return tuple(grad.reshape(queries.shape) for grad in settle(grads))
 
 
 def body(queries, keys, values, out_grad, tile_lists):

time: 92.2 us -> 88.9 us (0.964)
  local copies, waits for them, and re-layouts: 3.97 us -> 0 us
    unnamed x7 -> x0, local copies, waits for them, and re-layouts: 3.97 us -> none
    pallas_call x0 -> x1, Pallas kernels: none -> 1.17 us  [settle(): pl.pallas_call(settle_kernel, out_shape=[pltpu.HBM(grad.shape, grad.dtype...]
where the time goes in v2:
time: 88.9 us; the launch traced here: 88.7 us
  Pallas kernels  88.1 us (99%)
    pallas_call x1, Pallas kernels, head_body(): pl.pallas_call(functools.partial(head_kernel, seq_count, tensor_count), o...  86.9 us

profile of v2, /device:TPU:0, one launch (start us, length us, event | category | flops | bytes accessed | tf_op | source)
XLA Modules:
  0.0 88.7 jit_solution(10977121296636134934)
XLA Ops:
  0.6 86.9 %shard_map.76 = (bf16[128,2048]{1,0:T(8,128)(2,1)S(1)}, bf16[128,2048]{1,0:T(8,128)(2,1)S(1)}, bf16[128,2048]{1,0:T(8,128)(2,1)S(1)}) custom-call(bf16[128,2048]{1,0:T(8,128)(2,1)} %bitcast.7, bf16[128,2048]{1,0:T(8,128)(2,1)} %bitcast.8, bf16[128,2048]{1,0:T(8,128)(2,1)} %bitcast.9, bf16[128,2048]{1,0:T(8,128)(2,1)} %bitcast.10, s32[8,12]{1,0:T(8,128)} %lists_hbm.1), custom_call_target="tpu_custom_call" | custom-call | tf_op jit(solution)/shard_map/pallas_call | solution.py:470
  87.6 1.2 %shard_map.77 = (bf16[128,2048]{1,0:T(8,128)(2,1)}, bf16[128,2048]{1,0:T(8,128)(2,1)}, bf16[128,2048]{1,0:T(8,128)(2,1)}) custom-call(bf16[128,2048]{1,0:T(8,128)(2,1)S(1)} %get-tuple-element.9.refs_0_, bf16[128,2048]{1,0:T(8,128)(2,1)S(1)} %get-tuple-element.10.refs_1_, bf16[128,2048]{1,0:T(8,128)(2,1)S(1)} %get-tuple-element.11.refs_2_), custom_call_target="tpu_custom_call" | custom-call | tf_op jit(solution)/shard_map/pallas_call | solution.py:452

commit v3 on v2

--- a/solution.py
+++ b/solution.py
@@ -140,7 +140,7 @@
 def partner_order(seq_count, tensor_count):
     order = []
     for step in range(seq_count):
-        reach = (seq_count // 2 + ((step + 1) // 2) * (2 * (step % 2) - 1)) % seq_count
+        reach = (seq_count // 2 + ((step + 1) // 2) * (1 - 2 * (step % 2))) % seq_count
         for turn in range(tensor_count):
             if reach or turn:
                 order.append((reach, turn))
@@ -158,8 +158,7 @@
     dq_hbm,
     dk_hbm,
     dv_hbm,
-    q_all,
-    k_all,
+    qk_all,
     v_all,
     g_all,
     lists_all,
@@ -210,16 +209,19 @@
         pltpu.make_async_copy(src, staged.at[which], local_sem.at[8 + which])
         for which, src in enumerate((q_hbm, k_hbm, g_hbm, v_hbm))
     ]
-    incoming = tuple(
-        (staged.at[which], dst) for which, dst in enumerate((q_all, k_all, g_all, v_all))
-    )
+    q_all, k_all = qk_all.at[0], qk_all.at[1]
+    incoming = {
+        0: (lambda cols: staged.at[pl.ds(0, 2), :, cols], lambda slot: qk_all.at[:, slot]),
+        2: (lambda cols: staged.at[2, :, cols], lambda slot: g_all.at[slot]),
+        3: (lambda cols: staged.at[3, :, cols], lambda slot: v_all.at[slot]),
+    }
     outgoing = ((dv_out, dv_hbm), (dq_out, dq_hbm), (dk_out, dk_hbm))
 
     def in_copy(which, seq_there, tensor_there, there):
         src, dst = incoming[which]
         return remote(
-            src.at[:, columns(there)],
-            dst.at[me],
+            src(columns(there)),
+            dst(me),
             in_send.at[which, there],
             in_recv.at[which, me],
             seq_there,
@@ -229,8 +231,8 @@
     def in_wait(which, seq_there, tensor_there, there):
         src, dst = incoming[which]
         remote(
-            src.at[:, columns(there)],
-            dst.at[there],
+            src(columns(there)),
+            dst(there),
             in_send.at[which, there],
             in_recv.at[which, there],
             seq_there,
@@ -239,7 +241,7 @@
 
     def in_local(which):
         src, dst = incoming[which]
-        return pltpu.make_async_copy(src.at[:, columns(me)], dst.at[me], local_sem.at[which])
+        return pltpu.make_async_copy(src(columns(me)), dst(me), local_sem.at[which])
 
     def out_copy(which, seq_there, tensor_there, there):
         src, dst = outgoing[which]
@@ -297,10 +299,9 @@
     for group in ((0, 1), (2,), (3,)):
         for which in group:
             staging[which].wait()
-            in_local(which).start()
+        in_local(group[0]).start()
         for partner in partners:
-            for which in group:
-                in_copy(which, *partner).start()
+            in_copy(group[0], *partner).start()
 
     own_list.wait()
     for turn in range(1, tensor_count):
@@ -317,11 +318,9 @@
     dv_sum[...] = jnp.zeros_like(dv_sum)
     dk_sum[...] = jnp.zeros_like(dk_sum)
 
-    for which in (0, 1):
-        in_local(which).wait()
+    in_local(0).wait()
     for partner in partners:
-        for which in (0, 1):
-            in_wait(which, *partner)
+        in_wait(0, *partner)
 
     def pair_rows(ref, index):
         return ref[pl.ds(2 * index, 2)].reshape(2 * TILE, DH)
@@ -473,8 +472,7 @@
         in_specs=[anywhere] * 5,
         out_specs=[anywhere] * 3,
         scratch_shapes=[
-            per_tile,
-            per_tile,
+            pltpu.VMEM((2, tiles, TILE, DH), jnp.bfloat16),
             per_tile,
             per_tile,
             pltpu.VMEM((tensor_count,) + tile_lists.shape, jnp.int32),

time: 88.9 us -> 88.1 us (level)
  Pallas kernels: 88.1 us -> 86.6 us
    pallas_call x1, Pallas kernels: 86.9 us -> 85.4 us  [head_body(): pl.pallas_call(functools.partial(head_kernel, seq_count, tensor_count), o...]
where the time goes in v3:
time: 88.1 us; the launch traced here: 87.2 us
  Pallas kernels  86.6 us (98%)
    pallas_call x1, Pallas kernels, head_body(): pl.pallas_call(functools.partial(head_kernel, seq_count, tensor_count), o...  85.4 us

profile of v3, /device:TPU:0, one launch (start us, length us, event | category | flops | bytes accessed | tf_op | source)
XLA Modules:
  0.0 87.2 jit_solution(15023351936222531956)
XLA Ops:
  0.6 85.4 %shard_map.76 = (bf16[128,2048]{1,0:T(8,128)(2,1)S(1)}, bf16[128,2048]{1,0:T(8,128)(2,1)S(1)}, bf16[128,2048]{1,0:T(8,128)(2,1)S(1)}) custom-call(bf16[128,2048]{1,0:T(8,128)(2,1)} %bitcast.7, bf16[128,2048]{1,0:T(8,128)(2,1)} %bitcast.8, bf16[128,2048]{1,0:T(8,128)(2,1)} %bitcast.9, bf16[128,2048]{1,0:T(8,128)(2,1)} %bitcast.10, s32[8,12]{1,0:T(8,128)} %lists_hbm.1), custom_call_target="tpu_custom_call" | custom-call | tf_op jit(solution)/shard_map/pallas_call | solution.py:469
  86.0 1.2 %shard_map.77 = (bf16[128,2048]{1,0:T(8,128)(2,1)}, bf16[128,2048]{1,0:T(8,128)(2,1)}, bf16[128,2048]{1,0:T(8,128)(2,1)}) custom-call(bf16[128,2048]{1,0:T(8,128)(2,1)S(1)} %get-tuple-element.9.refs_0_, bf16[128,2048]{1,0:T(8,128)(2,1)S(1)} %get-tuple-element.10.refs_1_, bf16[128,2048]{1,0:T(8,128)(2,1)S(1)} %get-tuple-element.11.refs_2_), custom_call_target="tpu_custom_call" | custom-call | tf_op jit(solution)/shard_map/pallas_call | solution.py:451

commit v4 on v3

--- a/solution.py
+++ b/solution.py
@@ -424,7 +424,7 @@
 
     lax.fori_loop(0, pairs, grad_pair_step, 0)
     dk_out[...] = dk_sum[...].astype(jnp.bfloat16).reshape(dk_out.shape)
-    for partner in partners:
+    for partner in partners[1::2] + partners[::2]:
         out_copy(2, *partner).start()
     out_local(1).start()
     out_local(2).start()

time: 88.1 us -> 89.4 us (1.015)
  Pallas kernels: 86.6 us -> 88.7 us
    pallas_call x1, Pallas kernels: 85.4 us -> 87.5 us  [head_body(): pl.pallas_call(functools.partial(head_kernel, seq_count, tensor_count), o...]
where the time goes in v4:
time: 89.4 us; the launch traced here: 89.3 us
  Pallas kernels  88.7 us (99%)
    pallas_call x1, Pallas kernels, head_body(): pl.pallas_call(functools.partial(head_kernel, seq_count, tensor_count), o...  87.5 us

profile of v4, /device:TPU:0, one launch (start us, length us, event | category | flops | bytes accessed | tf_op | source)
XLA Modules:
  0.0 89.3 jit_solution(9250985008384226356)
XLA Ops:
  0.6 87.5 %shard_map.76 = (bf16[128,2048]{1,0:T(8,128)(2,1)S(1)}, bf16[128,2048]{1,0:T(8,128)(2,1)S(1)}, bf16[128,2048]{1,0:T(8,128)(2,1)S(1)}) custom-call(bf16[128,2048]{1,0:T(8,128)(2,1)} %bitcast.7, bf16[128,2048]{1,0:T(8,128)(2,1)} %bitcast.8, bf16[128,2048]{1,0:T(8,128)(2,1)} %bitcast.9, bf16[128,2048]{1,0:T(8,128)(2,1)} %bitcast.10, s32[8,12]{1,0:T(8,128)} %lists_hbm.1), custom_call_target="tpu_custom_call" | custom-call | tf_op jit(solution)/shard_map/pallas_call | solution.py:469
  88.1 1.2 %shard_map.77 = (bf16[128,2048]{1,0:T(8,128)(2,1)}, bf16[128,2048]{1,0:T(8,128)(2,1)}, bf16[128,2048]{1,0:T(8,128)(2,1)}) custom-call(bf16[128,2048]{1,0:T(8,128)(2,1)S(1)} %get-tuple-element.9.refs_0_, bf16[128,2048]{1,0:T(8,128)(2,1)S(1)} %get-tuple-element.10.refs_1_, bf16[128,2048]{1,0:T(8,128)(2,1)S(1)} %get-tuple-element.11.refs_2_), custom_call_target="tpu_custom_call" | custom-call | tf_op jit(solution)/shard_map/pallas_call | solution.py:451
